TPU v7x, 512 devices: a whole 4x8x8 slice. The times are simulated.
512 devices in a mesh: dp: 32 (over x, z), tp: 16 (over y, core).
Axes of the slice: x: 4, y: 8, z: 8, core: 2. Of those that a mesh axis runs over, the one named last changes fastest.
Arguments:
- queries: bfloat16 [1024, 128, 576], P(('dp', 'tp')), may hold values from -40 to 40
- latent_cache: bfloat16 [1024, 256, 576], P(('dp', 'tp')), may hold values from -5 to 5
- lengths: int32 [1024], P(('dp', 'tp')), may hold values from 1 to 256, 65536 in all
- value_weight: bfloat16 [128, 512, 128], P('tp'), may hold values from -0.25 to 0.25
- output_weight: bfloat16 [16384, 7168], P('tp', 'dp'), may hold values from -0.046875 to 0.046875
Outputs:
- attended: bfloat16 [1024, 7168], P(('dp', 'tp'))
All inputs are finite; a program needn't handle non-finite values. No bound on the sum of `lengths` on one device may be relied on, other than what follows from the above.
Results may differ from a plain program's by a relative error of at most 0.0065.
Values may be sent and summed in bfloat16 or wider, within the bound.
No kernel may reach another device: no remote copies, remote signals or barrier semaphores. Data moves between devices by JAX's collectives and lax.ppermute only.
A program may use at most 64 MiB of HBM per device.

v0:
```python
import jax
import jax.numpy as jnp
from jax import lax
from jax.sharding import PartitionSpec as P

score_scale = 192.0 ** (-0.5)


def local(queries, latent_cache, lengths, value_weight, output_weight):
    requests = queries.shape[0]
    groups = lax.axis_size("tp")
    columns = lax.axis_size("dp")
    latent_width = value_weight.shape[1]
    scores = (
        jnp.einsum("rhe,rje->rhj", queries, latent_cache, preferred_element_type=jnp.float32)
        * score_scale
    )
    alive_mask = lax.broadcasted_iota(jnp.int32, scores.shape, 2) < lengths[:, None, None]
    scores = jnp.where(alive_mask, scores, -1e30)
    row_max = jnp.max(scores, axis=2, keepdims=True)
    powers = jnp.exp(scores - row_max)
    weights = (powers / jnp.sum(powers, axis=2, keepdims=True)).astype(jnp.bfloat16)
    mixture = jnp.einsum("rhj,rje->rhe", weights, latent_cache, preferred_element_type=jnp.float32)
    latent = mixture[:, :, :latent_width].astype(jnp.bfloat16)
    swapped = lax.all_to_all(latent, "tp", split_axis=1, concat_axis=0, tiled=True)
    values = jnp.einsum("qhd,hde->qhe", swapped, value_weight, preferred_element_type=jnp.float32)
    values = values.astype(jnp.bfloat16).reshape(groups, requests, -1)
    everyone = lax.all_gather(values, "dp", axis=1, tiled=True)
    all_values = everyone.reshape(groups * columns * requests, -1)
    summed = lax.psum_scatter(
        jnp.dot(all_values, output_weight, preferred_element_type=jnp.float32),
        "tp",
        scatter_dimension=0,
        tiled=True,
    )
    rounded = summed.astype(jnp.bfloat16)
    return lax.all_to_all(rounded, "dp", split_axis=0, concat_axis=1, tiled=True)


def solution(mesh):
    return jax.shard_map(
        local,
        mesh=mesh,
        in_specs=(
            P(("dp", "tp"), None, None),
            P(("dp", "tp"), None, None),
            P(("dp", "tp")),
            P("tp", None, None),
            P("tp", "dp"),
        ),
        out_specs=P(("dp", "tp"), None),
        check_vma=False,
    )
```

profile of v0, /device:TPU:2, one launch (start us, length us, event | category | flops | bytes accessed | tf_op | source)
XLA Modules:
  0.0 203.4 jit_solution(8184634764328297941)
XLA Ops:
  6.5 0.0 copy-start
  6.5 0.0 all-gather.2.cloned.1.call-start
  6.5 1.5 fusion.3
  8.1 0.2 fusion.8
  8.3 1.6 fusion.5
  9.9 0.3 copy.16
  10.2 18.2 %all_to_all.37 = bf16[2,128,512]{2,0,1:T(2,128)(2,1)S(1)} all-to-all(bf16[2,128,512]{2,0,1:T(2,128)(2,1)S(1)} %copy.16), channel_id=1, replica_groups=mesh['dp'=32,'tp'=16] {'tp'}, dimensions={1} | all-to-all | bytes 524288 | tf_op jit(solution)/shard_map/all_to_all | solution.py:25
  28.4 0.2 copy.23
  28.6 0.1 all_to_all.30
  28.7 0.0 copy-done
  28.7 0.3 fusion.4
  29.0 0.6 copy.19
  29.7 0.0 all-gather.2.cloned.1.call-update
  29.7 0.0 copy-start.1
  29.7 0.0 reduce-scatter.2.cloned.1.call-start
  29.7 83.9 %all-gather.2.cloned.1.call-done = bf16[16,64,1024]{2,0,1:T(8,128)(2,1)} async-done(((bf16[16,2,1024]{2,0,1:T(8,128)(2,1)}), bf16[16,64,1024]{2,0,1:T(8,128)(2,1)}) %all-gather.2.cloned.1.call-update) | async-done | bytes 2097168 | tf_op jit(solution)/shard_map/all_gather | solution.py:28
  113.6 2.7 %copy.20 = bf16[16,64,1024]{2,1,0:T(8,128)(2,1)S(1)} copy(bf16[16,64,1024]{2,0,1:T(8,128)(2,1)} %all-gather.2.cloned.1.call-done) | data formatting | bytes 4194304 | tf_op jit(solution)/shard_map/all_gather | solution.py:28
  116.4 0.0 copy-done.1
  116.4 1.7 fusion.9
  118.1 0.0 reduce-scatter.2.cloned.1.call-update
  118.2 57.8 %reduce-scatter.2.cloned.1.call-done = f32[64,224]{1,0:T(8,128)} async-done(((f32[1024,224]{1,0:T(8,128)}), f32[64,224]{1,0:T(8,128)}) %reduce-scatter.2.cloned.1.call-update) | async-done | bytes 57360 | tf_op jit(solution)/shard_map/reduce_scatter | solution.py:30
  175.9 0.8 convert_element_type.16
  176.8 19.0 %all_to_all.38 = bf16[32,2,224]{2,1,0:T(2,128)(2,1)S(1)} all-to-all(bf16[32,2,224]{2,1,0:T(2,128)(2,1)S(1)} %all_to_all.31), channel_id=1, replica_groups=mesh['dp'=32,'tp'=16] {'dp'}, dimensions={0} | all-to-all | bytes 57344 | tf_op jit(solution)/shard_map/all_to_all | solution.py:37
  195.8 0.7 all_to_all.34
  (5 shorter events, 0.1 us)
Async XLA Ops:
  6.5 22.1 %copy-start = (bf16[8,512,128]{2,1,0:T(8,128)(2,1)S(1)}, bf16[8,512,128]{2,1,0:T(8,128)(2,1)}, u32[]{:S(2)}) copy-start(bf16[8,512,128]{2,1,0:T(8,128)(2,1)} %param.8) | copy-start | bytes 3145732
  6.5 107.1 %all-gather.2.cloned.1.call-start = ((), (), s32[]{:S(2)}) async-start(), calls=%async_computation.3 | async-start | bytes 2162688 | tf_op jit(solution)/shard_map/all_gather | solution.py:28
  29.7 86.7 %copy-start.1 = (bf16[1024,224]{0,1:T(8,128)(2,1)S(1)}, bf16[1024,224]{0,1:T(8,128)(2,1)}, u32[]{:S(2)}) copy-start(bf16[1024,224]{0,1:T(8,128)(2,1)} %param.9) | copy-start | bytes 1376260
  29.7 146.2 %reduce-scatter.2.cloned.1.call-start = ((), (), s32[]{:S(2)}) async-start(), calls=%async_computation.4 | async-start | bytes 1114112 | tf_op jit(solution)/shard_map/reduce_scatter | solution.py:30
Sparse Core Ops, SparseCore 0:
  29.8 83.7 all-gather.1
  118.3 57.6 reduce-scatter.1
where the time goes:
time: 204 us; the launch traced here: 203 us
  waiting for transfers between devices  142 us (70%)
  blocking collectives  37.2 us (18%)
  between operations  13.5 us (7%)
  matrix products  5.14 us (3%)
  local copies, waits for them, and re-layouts  4.78 us (2%)
    all_gather x1, waiting for transfers between devices, local(): everyone = lax.all_gather(values, 'dp', axis=1, tiled=True)  83.9 us
    reduce_scatter x1, waiting for transfers between devices, local(): lax.psum_scatter(jnp.dot(all_values, output_weight, preferred_element_typ...  57.8 us
    all_to_all x1, blocking collectives, local(): lax.all_to_all(rounded, 'dp', split_axis=0, concat_axis=1, tiled=True)  19 us
    all_to_all x1, blocking collectives, local(): lax.all_to_all(latent, 'tp', split_axis=1, concat_axis=0, tiled=True)  18.2 us
  transfers between devices with their start and end apart: 2, of which 2 were waited for; matrix products, arithmetic and copies ran while one was open for 0% of the time, Pallas kernels for 0%

commit v1 on v0

--- a/solution.py
+++ b/solution.py
@@ -2,6 +2,7 @@
 import jax.numpy as jnp
 from jax import lax
 from jax.sharding import PartitionSpec as P
+from jax.lax import all_to_all, axis_size
 
 score_scale = 192.0 ** (-0.5)
 
@@ -25,7 +26,11 @@
     swapped = lax.all_to_all(latent, "tp", split_axis=1, concat_axis=0, tiled=True)
     values = jnp.einsum("qhd,hde->qhe", swapped, value_weight, preferred_element_type=jnp.float32)
     values = values.astype(jnp.bfloat16).reshape(groups, requests, -1)
-    everyone = lax.all_gather(values, "dp", axis=1, tiled=True)
+    nd = axis_size("dp")
+    in_order = []
+    for tick in range(values.ndim):
+        in_order.append(nd if tick == 1 else 1)
+    everyone = all_to_all(jnp.tile(values, in_order), "dp", split_axis=1, concat_axis=1, tiled=True)
     all_values = everyone.reshape(groups * columns * requests, -1)
     summed = lax.psum_scatter(
         jnp.dot(all_values, output_weight, preferred_element_type=jnp.float32),

time: 204 us -> 177 us (0.87)
  waiting for transfers between devices: 142 us -> 54.4 us
  blocking collectives: 37.2 us -> 99.7 us
    all_gather x1 -> x0, waiting for transfers between devices: 83.9 us -> none  [local(): everyone = lax.all_gather(values, 'dp', axis=1, tiled=True)]
    all_to_all x0 -> x1, blocking collectives: none -> 62.7 us  [local(): all_to_all(jnp.tile(values, in_order), 'dp', split_axis=1, concat_axis=1,...]
    reduce_scatter x1, waiting for transfers between devices: 57.8 us -> 54.3 us  [local(): lax.psum_scatter(jnp.dot(all_values, output_weight, preferred_element_typ...]
    all_gather x1 -> x0, local copies, waits for them, and re-layouts: 2.74 us -> none  [local(): everyone = lax.all_gather(values, 'dp', axis=1, tiled=True)]
  transfers between devices with their start and end apart: 2 -> 1, of which waited for: 2 -> 1; matrix products, arithmetic and copies ran while one was open for 0% -> 0% of each run, Pallas kernels for 0% -> 0%
where the time goes in v1:
time: 177 us
  blocking collectives  99.7 us (56%)
  waiting for transfers between devices  54.4 us (31%)
  between operations  13.5 us (8%)
  matrix products  5.14 us (3%)
  local copies, waits for them, and re-layouts  2.82 us (2%)
    all_to_all x1, blocking collectives, local(): all_to_all(jnp.tile(values, in_order), 'dp', split_axis=1, concat_axis=1,...  62.7 us
    reduce_scatter x1, waiting for transfers between devices, local(): lax.psum_scatter(jnp.dot(all_values, output_weight, preferred_element_typ...  54.3 us
    all_to_all x1, blocking collectives, local(): lax.all_to_all(rounded, 'dp', split_axis=0, concat_axis=1, tiled=True)  18.8 us
    all_to_all x1, blocking collectives, local(): lax.all_to_all(latent, 'tp', split_axis=1, concat_axis=0, tiled=True)  18.2 us
  transfers between devices with their start and end apart: 1, of which 1 were waited for; matrix products, arithmetic and copies ran while one was open for 0% of the time, Pallas kernels for 0%

profile of v1, /device:TPU:2, one launch (start us, length us, event | category | flops | bytes accessed | tf_op | source)
XLA Modules:
  0.0 176.5 jit_solution(12853668163846815299)
XLA Ops:
  6.5 0.0 copy-start
  6.5 0.0 reduce-scatter.2.cloned.1.call-start
  6.5 1.5 fusion.3
  8.1 0.2 fusion.8
  8.3 1.6 fusion.5
  9.9 0.3 copy.16
  10.2 18.2 %all_to_all.42 = bf16[2,128,512]{2,0,1:T(2,128)(2,1)S(1)} all-to-all(bf16[2,128,512]{2,0,1:T(2,128)(2,1)S(1)} %copy.16), channel_id=1, replica_groups=mesh['dp'=32,'tp'=16] {'tp'}, dimensions={1} | all-to-all | bytes 524288 | tf_op jit(solution)/shard_map/all_to_all | solution.py:26
  28.4 0.2 copy.23
  28.6 0.1 all_to_all.33
  28.7 0.0 copy-done
  28.7 0.3 fusion.4
  29.1 0.2 tile.11
  29.3 62.7 %all_to_all.43 = bf16[16,64,1024]{2,0,1:T(8,128)(2,1)S(1)} all-to-all(bf16[16,64,1024]{2,0,1:T(8,128)(2,1)S(1)} %bitcast.21), channel_id=1, replica_groups=mesh['dp'=32,'tp'=16] {'dp'}, dimensions={1} | all-to-all | bytes 4194304 | tf_op jit(solution)/shard_map/all_to_all | solution.py:33
  92.0 0.0 copy-start.1
  92.0 1.2 copy.20
  93.2 0.0 copy-done.1
  93.2 1.7 fusion.9
  94.9 0.0 reduce-scatter.2.cloned.1.call-update
  94.9 54.3 %reduce-scatter.2.cloned.1.call-done = f32[64,224]{1,0:T(8,128)} async-done(((f32[1024,224]{1,0:T(8,128)}), f32[64,224]{1,0:T(8,128)}) %reduce-scatter.2.cloned.1.call-update) | async-done | bytes 57360 | tf_op jit(solution)/shard_map/reduce_scatter | solution.py:35
  149.3 0.8 convert_element_type.16
  150.1 18.8 %all_to_all.44 = bf16[32,2,224]{2,1,0:T(2,128)(2,1)S(1)} all-to-all(bf16[32,2,224]{2,1,0:T(2,128)(2,1)S(1)} %all_to_all.35), channel_id=1, replica_groups=mesh['dp'=32,'tp'=16] {'dp'}, dimensions={0} | all-to-all | bytes 57344 | tf_op jit(solution)/shard_map/all_to_all | solution.py:42
  168.9 0.7 all_to_all.38
  (6 shorter events, 0.1 us)
Async XLA Ops:
  6.5 22.1 %copy-start = (bf16[8,512,128]{2,1,0:T(8,128)(2,1)S(1)}, bf16[8,512,128]{2,1,0:T(8,128)(2,1)}, u32[]{:S(2)}) copy-start(bf16[8,512,128]{2,1,0:T(8,128)(2,1)} %param.8) | copy-start | bytes 3145732
  6.5 142.7 %reduce-scatter.2.cloned.1.call-start = ((), (), s32[]{:S(2)}) async-start(), calls=%async_computation.4 | async-start | bytes 1114112 | tf_op jit(solution)/shard_map/reduce_scatter | solution.py:35
  92.0 1.2 copy-start.1
Sparse Core Ops, SparseCore 0:
  95.0 54.1 reduce-scatter.1
